TPU v7x, 512 devices: a whole 4x8x8 slice. The times are simulated.
512 devices in a mesh: row: 16 (over z, core), col: 32 (over x, y).
Axes of the slice: x: 4, y: 8, z: 8, core: 2. Of those that a mesh axis runs over, the one named last changes fastest.
Arguments:
- tokens: bfloat16 [512, 8192], P('col', 'row'), may hold values from -24 to 24
- scales: float32 [8192], P('row'), may hold values from 0.25 to 4
- gate_weight: bfloat16 [8192, 16384], P('row', 'col'), may hold values from -0.0625 to 0.0625
- up_weight: bfloat16 [8192, 16384], P('row', 'col'), may hold values from -0.0625 to 0.0625
- down_weight: bfloat16 [16384, 8192], P('col', 'row'), may hold values from -0.046875 to 0.046875
- gate_mask: int32 [64, 128], P('row', 'col'), may hold values 0 or 1
- up_mask: int32 [64, 128], P('row', 'col'), may hold values 0 or 1
- down_mask: int32 [128, 64], P('col', 'row'), may hold values 0 or 1
- cotangent: bfloat16 [512, 8192], P('col', 'row'), may hold values from -4 to 4
Outputs:
- output: bfloat16 [512, 8192], P('col', 'row')
- input_grad: bfloat16 [512, 8192], P('col', 'row')
- gate_grad: bfloat16 [8192, 16384], P('row', 'col')
- up_grad: bfloat16 [8192, 16384], P('row', 'col')
- down_grad: bfloat16 [16384, 8192], P('col', 'row')
Inputs may be any that keep to these rules, and one draw needn't show every extreme that they name: gate_mask is 1 where a 128 x 128 tile of gate_weight is kept and 0 where it is pruned. up_mask is 1 where a tile of up_weight is kept and 0 where it is pruned. down_mask is 1 where a tile of down_weight is kept and 0 where it is pruned.
All inputs are finite; a program needn't handle non-finite values. No bound on the sum of `gate_mask` or of `up_mask` or of `down_mask` on one device may be relied on, other than what follows from the above.
Results may differ from a plain program's by a relative error of at most 0.039.
Values may be sent and summed in bfloat16 or wider, within the bound.
No kernel may reach another device: no remote copies, remote signals or barrier semaphores. Data moves between devices by JAX's collectives and lax.ppermute only.
A program may use at most 64 MiB of HBM per device.

v0:
```python
import jax
import jax.numpy as jnp
from jax import lax
from jax.sharding import PartitionSpec as P

D = 8192
TILE = 128
clip_ratio = 1.5


def expand(mask):
    return jnp.repeat(jnp.repeat(mask, TILE, axis=0), TILE, axis=1).astype(jnp.float32)


def contract_last(left, right):
    return lax.dot_general(
        left, right, (((1,), (1,)), ((), ())), preferred_element_type=jnp.float32
    )


def contract_first(left, right):
    return lax.dot_general(
        left, right, (((0,), (0,)), ((), ())), preferred_element_type=jnp.float32
    )


def clip_tokens(smoothed, squares):
    limits = clip_ratio * jnp.sqrt(squares / D + 1e-06)[:, None]
    squashed = jnp.tanh(smoothed / limits)
    return (squashed, (limits * squashed).astype(jnp.bfloat16))


def swiglu_parts(gate_pre):
    sigmoid_gate = jax.nn.sigmoid(gate_pre)
    silu_gate = gate_pre * sigmoid_gate
    return (sigmoid_gate, silu_gate)


def swiglu_grads(hidden_grad, gate_pre, up_pre):
    sigmoid_gate, silu_gate = swiglu_parts(gate_pre)
    gate_dir = (
        hidden_grad * up_pre * sigmoid_gate * (1.0 + gate_pre * (1.0 - sigmoid_gate))
    ).astype(jnp.bfloat16)
    up_dir = (hidden_grad * silu_gate).astype(jnp.bfloat16)
    return jnp.concatenate([gate_dir, up_dir], axis=1)


def per_device(
    tokens, scales, gate_weight, up_weight, down_weight, gate_mask, up_mask, down_mask, cotangent
):
    hidden_width = gate_weight.shape[1]
    gate_keep = expand(gate_mask)
    up_keep = expand(up_mask)
    down_keep = expand(down_mask)
    gate_kept = (scales[:, None] * gate_weight.astype(jnp.float32) * gate_keep).astype(jnp.bfloat16)
    up_kept = (scales[:, None] * up_weight.astype(jnp.float32) * up_keep).astype(jnp.bfloat16)
    down_kept = down_weight * down_keep.astype(jnp.bfloat16)
    both_kept = jnp.concatenate([gate_kept, up_kept], axis=1)
    smoothed = tokens.astype(jnp.float32) / scales
    squares = lax.psum(jnp.sum(smoothed * smoothed, axis=1), "row")
    squashed, quantized = clip_tokens(smoothed, squares)
    quantized_all = lax.all_gather(quantized, "col", axis=0, tiled=True)
    picked = quantized_all
    gate_up = lax.psum(
        jnp.dot(picked, both_kept, preferred_element_type=jnp.float32).astype(jnp.bfloat16), "row"
    ).astype(jnp.float32)
    gate_pre = gate_up[:, :hidden_width]
    up_pre = gate_up[:, hidden_width:]
    sigmoid_gate, silu_gate = swiglu_parts(gate_pre)
    hidden_all = (silu_gate * up_pre).astype(jnp.bfloat16)
    picked = hidden_all
    output = lax.psum_scatter(
        jnp.dot(picked, down_kept, preferred_element_type=jnp.float32).astype(jnp.bfloat16),
        "col",
        scatter_dimension=0,
        tiled=True,
    )
    cotangent_all = lax.all_gather(cotangent, "col", axis=0, tiled=True)
    down_grad = (contract_first(hidden_all, cotangent_all) * down_keep).astype(jnp.bfloat16)
    picked = cotangent_all
    hidden_grad = lax.psum(contract_last(picked, down_kept).astype(jnp.bfloat16), "row").astype(
        jnp.float32
    )
    both_dirs_all = swiglu_grads(hidden_grad, gate_pre, up_pre)
    picked = both_dirs_all
    quant_grad = lax.psum_scatter(
        contract_last(picked, both_kept).astype(jnp.bfloat16),
        "col",
        scatter_dimension=0,
        tiled=True,
    ).astype(jnp.float32)
    input_grad = (quant_grad * (1.0 - squashed * squashed) / scales).astype(jnp.bfloat16)
    weight_product = contract_first(quantized_all, both_dirs_all)
    gate_grad = (scales[:, None] * weight_product[:, :hidden_width] * gate_keep).astype(
        jnp.bfloat16
    )
    up_grad = (scales[:, None] * weight_product[:, hidden_width:] * up_keep).astype(jnp.bfloat16)
    return (output, input_grad, gate_grad, up_grad, down_grad)


def solution(mesh):
    placed = (
        P("col", "row"),
        P("row"),
        P("row", "col"),
        P("row", "col"),
        P("col", "row"),
        P("row", "col"),
        P("row", "col"),
        P("col", "row"),
        P("col", "row"),
    )
    return jax.shard_map(
        per_device,
        mesh=mesh,
        in_specs=placed,
        out_specs=(
            P("col", "row"),
            P("col", "row"),
            P("row", "col"),
            P("row", "col"),
            P("col", "row"),
        ),
        check_vma=False,
    )
```

profile of v0, /device:TPU:16, one launch (start us, length us, event | category | flops | bytes accessed | tf_op | source)
XLA Modules:
  0.0 713.3 jit_solution(10551113524191224439)
XLA Ops:
  7.2 0.9 fusion.15
  8.1 32.0 %psum.21 = f32[16]{0:T(128)S(1)} all-reduce(f32[16]{0:T(128)S(1)} %fusion.15), channel_id=1, replica_groups=mesh['row'=16,'col'=32] {'row'}, use_global_device_ids=true, to_apply=%region_1.0 | all-reduce | flops 16 | bytes 128 | tf_op jit(solution)/shard_map/psum | solution.py:60
  40.1 0.7 convert_element_type.102
  40.8 0.7 convert_element_type.107
  41.5 0.7 convert_element_type.114
  42.2 0.8 multiply_convert_fusion.1
  43.0 50.1 %all_gather.6 = bf16[512,512]{1,0:T(8,128)(2,1)S(1)} all-gather(bf16[16,512]{1,0:T(8,128)(2,1)S(1)} %multiply_convert_fusion.1), channel_id=1, replica_groups=mesh['row'=16,'col'=32] {'col'}, dimensions={0}, use_global_device_ids=true | all-gather | bytes 540672 | tf_op jit(solution)/shard_map/all_gather | solution.py:62
  93.1 47.0 %all_gather.7 = bf16[512,512]{1,0:T(8,128)(2,1)S(1)} all-gather(bf16[16,512]{1,0:T(8,128)(2,1)} %param.17), channel_id=1, replica_groups=mesh['row'=16,'col'=32] {'col'}, dimensions={0}, use_global_device_ids=true | all-gather | bytes 540672 | tf_op jit(solution)/shard_map/all_gather | solution.py:78
  140.7 1.3 fusion.1
  142.0 0.6 broadcast_in_dim.26
  143.7 0.8 copy-done.9
  144.6 1.7 convolution_convert_fusion
  146.4 114.4 %all-reduce.3.cloned.1.call-done = (bf16[512,1024]{1,0:T(8,128)(2,1)}, bf16[512,512]{1,0:T(8,128)(2,1)}) async-done(((bf16[512,1024]{1,0:T(8,128)(2,1)}, bf16[512,512]{1,0:T(8,128)(2,1)}), (bf16[512,1024]{1,0:T(8,128)(2,1)}, bf16[512,512]{1,0:T(8,128)(2,1)})) %all-reduce.3.cloned.1.call-update) | async-done | bytes 1572880 | tf_op jit(solution)/shard_map/psum | solution.py:64
  260.8 1.5 convert_element_type.112
  262.4 1.4 fusion.4
  263.8 0.8 copy-done.3
  264.8 1.6 convolution_convert_fusion.3
  266.4 2.5 convolution_convert_fusion.2
  269.0 2.6 fusion
  271.5 0.7 fusion.11
  272.3 1.2 fusion.7
  273.5 210.9 %reduce-scatter.5.cloned.1.call-done = bf16[16,512]{1,0:T(8,128)(2,1)} async-done(((bf16[512,512]{1,0:T(8,128)(2,1)}), bf16[16,512]{1,0:T(8,128)(2,1)}) %reduce-scatter.5.cloned.1.call-update) | async-done | bytes 16400 | tf_op jit(solution)/shard_map/reduce_scatter | solution.py:86
  484.5 1.4 divide_convert_fusion
  485.9 220.9 %reduce-scatter.3.cloned.1.call-done = bf16[16,512]{1,0:T(8,128)(2,1)} async-done(((bf16[512,512]{1,0:T(8,128)(2,1)}), bf16[16,512]{1,0:T(8,128)(2,1)}) %reduce-scatter.3.cloned.1.call-update) | async-done | bytes 16400 | tf_op jit(solution)/shard_map/reduce_scatter | solution.py:72
  (45 shorter events, 2.2 us)
Async XLA Ops:
  7.2 133.6 %copy-start.16 = (bf16[512,512]{1,0:T(8,128)(2,1)S(1)}, bf16[512,512]{1,0:T(8,128)(2,1)}, u32[]{:S(2)}) copy-start(bf16[512,512]{1,0:T(8,128)(2,1)} %param.13) | copy-start | bytes 1572868
  7.2 253.6 %all-reduce.3.cloned.1.call-start = ((), (), s32[]{:S(2)}) async-start(), calls=%async_computation.4 | async-start | bytes 3145728 | tf_op jit(solution)/shard_map/psum | solution.py:64
  93.1 50.6 %copy-start = (bf16[512,512]{1,0:T(8,128)(2,1)}, bf16[512,512]{1,0:T(8,128)(2,1)S(1)}, u32[]{:S(2)}) copy-start(bf16[512,512]{1,0:T(8,128)(2,1)S(1)} %all_gather.6) | copy-start | bytes 1572868
  140.1 1.9 copy-start.2
  142.0 1.3 copy-start.7
  142.0 1.3 copy-start.8
  142.0 1.3 copy-start.15
  143.6 0.8 copy-start.9
  143.6 1.0 copy-start.11
  146.3 338.1 %reduce-scatter.5.cloned.1.call-start = ((), (), s32[]{:S(2)}) async-start(), calls=%async_computation.3 | async-start | bytes 540672 | tf_op jit(solution)/shard_map/reduce_scatter | solution.py:86
  260.8 1.5 copy-start.13
  262.3 2.4 copy-start.10
  262.4 2.4 copy-start.12
  263.8 0.8 copy-start.3
  263.8 1.0 copy-start.5
  266.4 440.4 %reduce-scatter.3.cloned.1.call-start = ((), (), s32[]{:S(2)}) async-start(), calls=%async_computation.2 | async-start | bytes 540672 | tf_op jit(solution)/shard_map/reduce_scatter | solution.py:72
  268.9 2.6 copy-start.1
  268.9 2.6 copy-start.4
  268.9 2.6 copy-start.6
  272.3 212.2 %copy-start.14 = (bf16[16,512]{1,0:T(8,128)(2,1)S(1)}, bf16[16,512]{1,0:T(8,128)(2,1)}, u32[]{:S(2)}) copy-start(bf16[16,512]{1,0:T(8,128)(2,1)} %param.9) | copy-start | bytes 49156
Sparse Core Ops, SparseCore 0:
  146.4 114.3 all-reduce.2
  266.5 217.9 reduce-scatter.4
  489.4 217.3 reduce-scatter.2
where the time goes:
time: 714 us; the launch traced here: 713 us
  waiting for transfers between devices  546 us (76%)
  blocking collectives  129 us (18%)
  between operations  13.9 us (2%)
  matrix products  10.3 us (1%)
  other arithmetic  9.67 us (1%)
    reduce_scatter x1, waiting for transfers between devices, per_device(): lax.psum_scatter(jnp.dot(picked, down_kept, preferred_element_type=jnp.fl...  221 us
    reduce_scatter x1, waiting for transfers between devices, per_device(): lax.psum_scatter(contract_last(picked, both_kept).astype(jnp.bfloat16), '...  211 us
    psum x1, waiting for transfers between devices, per_device(): lax.psum(jnp.dot(picked, both_kept, preferred_element_type=jnp.float32).a...  114 us
    all_gather x1, blocking collectives, per_device(): quantized_all = lax.all_gather(quantized, 'col', axis=0, tiled=True)  50.1 us
    all_gather x1, blocking collectives, per_device(): cotangent_all = lax.all_gather(cotangent, 'col', axis=0, tiled=True)  47 us
    psum x1, blocking collectives, per_device(): squares = lax.psum(jnp.sum(smoothed * smoothed, axis=1), 'row')  32 us
  transfers between devices with their start and end apart: 3, of which 3 were waited for; matrix products, arithmetic and copies ran while one was open for 1% of the time, Pallas kernels for 0%

commit v1 on v0

--- a/solution.py
+++ b/solution.py
@@ -61,8 +61,12 @@
     squashed, quantized = clip_tokens(smoothed, squares)
     quantized_all = lax.all_gather(quantized, "col", axis=0, tiled=True)
     picked = quantized_all
-    gate_up = lax.psum(
-        jnp.dot(picked, both_kept, preferred_element_type=jnp.float32).astype(jnp.bfloat16), "row"
+    gate_up = jnp.sum(
+        lax.all_gather(
+            jnp.dot(picked, both_kept, preferred_element_type=jnp.float32).astype(jnp.bfloat16),
+            "row",
+        ),
+        axis=0,
     ).astype(jnp.float32)
     gate_pre = gate_up[:, :hidden_width]
     up_pre = gate_up[:, hidden_width:]

time: 714 us -> 759 us (1.063)
  waiting for transfers between devices: 546 us -> 577 us
  other arithmetic: 9.67 us -> 21.5 us
    all_gather x0 -> x1, waiting for transfers between devices: none -> 42.1 us  [per_device(): lax.all_gather(jnp.dot(picked, both_kept, preferred_element_type=jnp.floa...]
    psum x1, waiting for transfers between devices: 114 us -> 103 us  [per_device(): lax.psum(contract_last(picked, down_kept).astype(jnp.bfloat16), 'row')]
    reduce_sum x0 -> x1, other arithmetic: none -> 9.33 us  [per_device(): jnp.sum(lax.all_gather(jnp.dot(picked, both_kept, preferred_element_type=...]
  transfers between devices with their start and end apart: 3 -> 4, of which waited for: 3 -> 4; matrix products, arithmetic and copies ran while one was open for 1% -> 3% of each run, Pallas kernels for 0% -> 0%
where the time goes in v1:
time: 759 us
  waiting for transfers between devices  577 us (76%)
  blocking collectives  129 us (17%)
  other arithmetic  21.5 us (3%)
  between operations  14 us (2%)
  matrix products  10.5 us (1%)
    reduce_scatter x1, waiting for transfers between devices, per_device(): lax.psum_scatter(jnp.dot(picked, down_kept, preferred_element_type=jnp.fl...  221 us
    reduce_scatter x1, waiting for transfers between devices, per_device(): lax.psum_scatter(contract_last(picked, both_kept).astype(jnp.bfloat16), '...  211 us
    psum x1, waiting for transfers between devices, per_device(): lax.psum(contract_last(picked, down_kept).astype(jnp.bfloat16), 'row')  103 us
    all_gather x1, blocking collectives, per_device(): quantized_all = lax.all_gather(quantized, 'col', axis=0, tiled=True)  50.1 us
    all_gather x1, blocking collectives, per_device(): cotangent_all = lax.all_gather(cotangent, 'col', axis=0, tiled=True)  47.2 us
    all_gather x1, waiting for transfers between devices, per_device(): lax.all_gather(jnp.dot(picked, both_kept, preferred_element_type=jnp.floa...  42.1 us
    psum x1, blocking collectives, per_device(): squares = lax.psum(jnp.sum(smoothed * smoothed, axis=1), 'row')  32 us
  transfers between devices with their start and end apart: 4, of which 4 were waited for; matrix products, arithmetic and copies ran while one was open for 3% of the time, Pallas kernels for 0%

profile of v1, /device:TPU:16, one launch (start us, length us, event | category | flops | bytes accessed | tf_op | source)
XLA Modules:
  0.0 758.5 jit_solution(18401673958982274752)
XLA Ops:
  7.2 0.8 convert_element_type.104
  8.7 0.8 fusion.15
  9.5 32.0 %psum.14 = f32[16]{0:T(128)S(1)} all-reduce(f32[16]{0:T(128)S(1)} %fusion.15), channel_id=1, replica_groups=mesh['row'=16,'col'=32] {'row'}, use_global_device_ids=true, to_apply=%region_1.0 | all-reduce | flops 16 | bytes 128 | tf_op jit(solution)/shard_map/psum | solution.py:60
  41.6 0.8 multiply_convert_fusion.1
  42.4 50.1 %all_gather.12 = bf16[512,512]{1,0:T(8,128)(2,1)S(1)} all-gather(bf16[16,512]{1,0:T(8,128)(2,1)S(1)} %multiply_convert_fusion.1), channel_id=1, replica_groups=mesh['row'=16,'col'=32] {'col'}, dimensions={0}, use_global_device_ids=true | all-gather | bytes 540672 | tf_op jit(solution)/shard_map/all_gather | solution.py:62
  95.0 1.7 convolution_convert_fusion
  96.8 47.2 %all_gather.15 = bf16[512,512]{1,0:T(8,128)(2,1)S(1)} all-gather(bf16[16,512]{1,0:T(8,128)(2,1)S(1)} %copy-done.16), channel_id=1, replica_groups=mesh['row'=16,'col'=32] {'col'}, dimensions={0}, use_global_device_ids=true | all-gather | bytes 540672 | tf_op jit(solution)/shard_map/all_gather | solution.py:82
  144.8 0.8 copy-done
  145.6 1.3 fusion.1
  146.9 42.1 %all-gather.3.cloned.1.call-done = bf16[8192,1024]{1,0:T(8,128)(2,1)} async-done(((bf16[512,1024]{1,0:T(8,128)(2,1)}), bf16[8192,1024]{1,0:T(8,128)(2,1)}) %all-gather.3.cloned.1.call-update) | async-done | bytes 16777232 | tf_op jit(solution)/shard_map/all_gather | solution.py:65
  189.0 9.3 %reduce_sum.22 = bf16[512,1024]{1,0:T(8,128)(2,1)S(1)} reduce(bf16[16,512,1024]{2,1,0:T(8,128)(2,1)} %bitcast.36, bf16[]{:T(256)} %constant.12.clone.1), dimensions={0}, to_apply=%region_2.0 | reduce | flops 7864320 | bytes 17825794 | tf_op jit(solution)/shard_map/reduce_sum | solution.py:64
  198.4 1.3 copy.14
  199.7 2.8 convert_element_type.114
  202.5 103.2 %all-reduce.2.cloned.1.call-done = bf16[512,512]{0,1:T(8,128)(2,1)} async-done(((bf16[512,512]{0,1:T(8,128)(2,1)}), bf16[512,512]{0,1:T(8,128)(2,1)}) %all-reduce.2.cloned.1.call-update) | async-done | bytes 524304 | tf_op jit(solution)/shard_map/psum | solution.py:85
  305.8 3.2 fusion.4
  309.0 0.8 copy-done.6
  310.0 1.6 convolution_convert_fusion.3
  311.7 2.5 convolution_convert_fusion.2
  314.2 2.2 fusion.11
  316.4 1.2 fusion
  317.7 1.2 fusion.7
  318.9 211.0 %reduce-scatter.5.cloned.1.call-done = bf16[16,512]{1,0:T(8,128)(2,1)} async-done(((bf16[512,512]{1,0:T(8,128)(2,1)}), bf16[16,512]{1,0:T(8,128)(2,1)}) %reduce-scatter.5.cloned.1.call-update) | async-done | bytes 16400 | tf_op jit(solution)/shard_map/reduce_scatter | solution.py:90
  529.9 1.4 divide_convert_fusion
  531.3 220.7 %reduce-scatter.3.cloned.1.call-done = bf16[16,512]{1,0:T(8,128)(2,1)} async-done(((bf16[512,512]{1,0:T(8,128)(2,1)}), bf16[16,512]{1,0:T(8,128)(2,1)}) %reduce-scatter.3.cloned.1.call-update) | async-done | bytes 16400 | tf_op jit(solution)/shard_map/reduce_scatter | solution.py:76
  (54 shorter events, 4.4 us)
Async XLA Ops:
  7.2 86.5 %copy-start.15 = (f32[512]{0:T(512)S(1)}, f32[512]{0:T(512)}, u32[]{:S(2)}) copy-start(f32[512]{0:T(512)} %param.10) | copy-start | bytes 6148
  7.2 86.5 %copy-start.8 = (bf16[512,512]{1,0:T(8,128)(2,1)S(1)}, bf16[512,512]{1,0:T(8,128)(2,1)}, u32[]{:S(2)}) copy-start(bf16[512,512]{1,0:T(8,128)(2,1)} %param.11) | copy-start | bytes 1572868
  7.2 86.5 %copy-start.9 = (bf16[512,512]{1,0:T(8,128)(2,1)S(1)}, bf16[512,512]{1,0:T(8,128)(2,1)}, u32[]{:S(2)}) copy-start(bf16[512,512]{1,0:T(8,128)(2,1)} %param.12) | copy-start | bytes 1572868
  7.2 181.8 %all-gather.3.cloned.1.call-start = ((), (), s32[]{:S(2)}) async-start(), calls=%async_computation.5 | async-start | bytes 17825792 | tf_op jit(solution)/shard_map/all_gather | solution.py:65
  92.4 1.6 copy-start.2
  94.0 0.8 copy-start.10
  94.0 1.0 copy-start.12
  95.0 1.8 copy-start.17
  95.0 1.8 copy-start.16
  96.7 48.9 %copy-start.18 = (bf16[512,512]{1,0:T(8,128)(2,1)S(1)}, bf16[512,512]{1,0:T(8,128)(2,1)}, u32[]{:S(2)}) copy-start(bf16[512,512]{1,0:T(8,128)(2,1)} %param.13) | copy-start | bytes 1572868
  96.7 209.0 %all-reduce.2.cloned.1.call-start = ((), (), s32[]{:S(2)}) async-start(), calls=%async_computation.3 | async-start | bytes 1048576 | tf_op jit(solution)/shard_map/psum | solution.py:85
  144.0 0.8 copy-start.3
  144.6 1.0 copy-start
  146.9 383.0 %reduce-scatter.5.cloned.1.call-start = ((), (), s32[]{:S(2)}) async-start(), calls=%async_computation.4 | async-start | bytes 540672 | tf_op jit(solution)/shard_map/reduce_scatter | solution.py:90
  305.8 4.2 copy-start.11
  305.8 4.2 copy-start.13
  309.0 0.8 copy-start.6
  309.0 1.0 copy-start.7
  310.0 1.7 copy-start.1
  311.6 440.4 %reduce-scatter.3.cloned.1.call-start = ((), (), s32[]{:S(2)}) async-start(), calls=%async_computation.2 | async-start | bytes 540672 | tf_op jit(solution)/shard_map/reduce_scatter | solution.py:76
  314.2 2.2 copy-start.4
  314.2 2.2 copy-start.5
  317.7 212.2 %copy-start.14 = (bf16[16,512]{1,0:T(8,128)(2,1)S(1)}, bf16[16,512]{1,0:T(8,128)(2,1)}, u32[]{:S(2)}) copy-start(bf16[16,512]{1,0:T(8,128)(2,1)} %param.9) | copy-start | bytes 49156
Sparse Core Ops, SparseCore 0:
  96.8 92.1 all-gather.2
  191.9 113.8 all-reduce.1
  311.7 218.1 reduce-scatter.4
  534.7 217.2 reduce-scatter.2

commit v2 on v0

--- a/solution.py
+++ b/solution.py
@@ -59,7 +59,9 @@
     smoothed = tokens.astype(jnp.float32) / scales
     squares = lax.psum(jnp.sum(smoothed * smoothed, axis=1), "row")
     squashed, quantized = clip_tokens(smoothed, squares)
-    quantized_all = lax.all_gather(quantized, "col", axis=0, tiled=True)
+    quantized_all = jnp.concatenate(
+        lax.all_to_all(jnp.stack([quantized] * lax.axis_size("col")), "col", 0, 0), axis=0
+    )
     picked = quantized_all
     gate_up = lax.psum(
         jnp.dot(picked, both_kept, preferred_element_type=jnp.float32).astype(jnp.bfloat16), "row"

time: 714 us -> 683 us (0.957)
  blocking collectives: 129 us -> 83.4 us
  starting transfers between devices: 0.12 us -> 10.2 us
    all_gather x1 -> x0, blocking collectives: 50.1 us -> none  [per_device(): quantized_all = lax.all_gather(quantized, 'col', axis=0, tiled=True)]
    all_to_all x0 -> x1, starting transfers between devices: none -> 10.1 us  [per_device(): lax.all_to_all(jnp.stack([quantized] * lax.axis_size('col')), 'col', 0, 0)]
  transfers between devices with their start and end apart: 3 -> 4, of which waited for: 3 -> 3; matrix products, arithmetic and copies ran while one was open for 1% -> 2% of each run, Pallas kernels for 0% -> 0%
where the time goes in v2:
time: 683 us; the launch traced here: 682 us
  waiting for transfers between devices  547 us (80%)
  blocking collectives  83.4 us (12%)
  between operations  13.9 us (2%)
  matrix products  12.6 us (2%)
  other arithmetic  10.7 us (2%)
  starting transfers between devices  10.2 us (1%)
    reduce_scatter x1, waiting for transfers between devices, per_device(): lax.psum_scatter(jnp.dot(picked, down_kept, preferred_element_type=jnp.fl...  221 us
    reduce_scatter x1, waiting for transfers between devices, per_device(): lax.psum_scatter(contract_last(picked, both_kept).astype(jnp.bfloat16), '...  210 us
    psum x1, waiting for transfers between devices, per_device(): lax.psum(jnp.dot(picked, both_kept, preferred_element_type=jnp.float32).a...  116 us
    all_gather x1, blocking collectives, per_device(): cotangent_all = lax.all_gather(cotangent, 'col', axis=0, tiled=True)  51.4 us
    psum x1, blocking collectives, per_device(): squares = lax.psum(jnp.sum(smoothed * smoothed, axis=1), 'row')  32 us
  transfers between devices with their start and end apart: 4, of which 3 were waited for; matrix products, arithmetic and copies ran while one was open for 2% of the time, Pallas kernels for 0%

profile of v2, /device:TPU:16, one launch (start us, length us, event | category | flops | bytes accessed | tf_op | source)
XLA Modules:
  0.0 682.1 jit_solution(1162408191164852506)
XLA Ops:
  7.2 0.9 fusion.15
  8.1 32.0 %psum.21 = f32[16]{0:T(128)S(1)} all-reduce(f32[16]{0:T(128)S(1)} %fusion.15), channel_id=1, replica_groups=mesh['row'=16,'col'=32] {'row'}, use_global_device_ids=true, to_apply=%region_1.0 | all-reduce | flops 16 | bytes 128 | tf_op jit(solution)/shard_map/psum | solution.py:60
  40.1 0.8 multiply_convert_fusion.1
  40.9 0.9 stack.2
  41.8 10.1 %all-to-all-start = ((bf16[32,16,512]{2,1,0:T(8,128)(2,1)}), bf16[32,16,512]{2,1,0:T(8,128)(2,1)}, u32[]{:S(2)}, u32[]{:S(2)}) async-start(bf16[32,16,512]{2,1,0:T(8,128)(2,1)} %stack.2), calls=%async_computation | async-start | bytes 1048576 | tf_op jit(solution)/shard_map/all_to_all | solution.py:63
  51.9 0.7 convert_element_type.102
  52.6 0.7 convert_element_type.107
  53.3 0.7 convert_element_type.114
  54.0 51.4 %all_gather.3 = bf16[512,512]{1,0:T(8,128)(2,1)S(1)} all-gather(bf16[16,512]{1,0:T(8,128)(2,1)} %param.17), channel_id=1, replica_groups=mesh['row'=16,'col'=32] {'col'}, dimensions={0}, use_global_device_ids=true | all-gather | bytes 540672 | tf_op jit(solution)/shard_map/all_gather | solution.py:80
  106.0 1.3 fusion.1
  108.6 1.3 fusion.8
  109.9 3.1 convolution_convert_fusion
  113.0 116.4 %all-reduce.3.cloned.1.call-done = (bf16[512,1024]{1,0:T(8,128)(2,1)}, bf16[512,512]{1,0:T(8,128)(2,1)}) async-done(((bf16[512,1024]{1,0:T(8,128)(2,1)}, bf16[512,512]{1,0:T(8,128)(2,1)}), (bf16[512,1024]{1,0:T(8,128)(2,1)}, bf16[512,512]{1,0:T(8,128)(2,1)})) %all-reduce.3.cloned.1.call-update) | async-done | bytes 1572880 | tf_op jit(solution)/shard_map/psum | solution.py:66
  229.4 1.5 convert_element_type.112
  231.0 1.5 fusion.4
  232.5 0.8 copy-done.1
  233.5 1.5 convolution_convert_fusion.3
  235.1 2.4 convolution_convert_fusion.2
  237.6 2.5 fusion
  240.1 1.8 fusion.11
  241.9 1.2 fusion.7
  243.2 210.0 %reduce-scatter.5.cloned.1.call-done = bf16[16,512]{1,0:T(8,128)(2,1)} async-done(((bf16[512,512]{1,0:T(8,128)(2,1)}), bf16[16,512]{1,0:T(8,128)(2,1)}) %reduce-scatter.5.cloned.1.call-update) | async-done | bytes 16400 | tf_op jit(solution)/shard_map/reduce_scatter | solution.py:88
  453.1 1.4 divide_convert_fusion
  454.6 221.0 %reduce-scatter.3.cloned.1.call-done = bf16[16,512]{1,0:T(8,128)(2,1)} async-done(((bf16[512,512]{1,0:T(8,128)(2,1)}), bf16[16,512]{1,0:T(8,128)(2,1)}) %reduce-scatter.3.cloned.1.call-update) | async-done | bytes 16400 | tf_op jit(solution)/shard_map/reduce_scatter | solution.py:74
  (39 shorter events, 2.2 us)
Async XLA Ops:
  7.2 98.8 %copy-start.12 = (bf16[512,512]{1,0:T(8,128)(2,1)S(1)}, bf16[512,512]{1,0:T(8,128)(2,1)}, u32[]{:S(2)}) copy-start(bf16[512,512]{1,0:T(8,128)(2,1)} %param.13) | copy-start | bytes 1572868
  41.8 68.1 %all-to-all-start = ((bf16[32,16,512]{2,1,0:T(8,128)(2,1)}), bf16[32,16,512]{2,1,0:T(8,128)(2,1)}, u32[]{:S(2)}, u32[]{:S(2)}) async-start(bf16[32,16,512]{2,1,0:T(8,128)(2,1)} %stack.2), calls=%async_computation | async-start | bytes 1048576 | tf_op jit(solution)/shard_map/all_to_all | solution.py:63
  51.9 177.6 %all-reduce.3.cloned.1.call-start = ((), (), s32[]{:S(2)}) async-start(), calls=%async_computation.5 | async-start | bytes 3145728 | tf_op jit(solution)/shard_map/psum | solution.py:66
  105.4 1.9 copy-start
  107.3 1.3 copy-start.5
  107.3 1.3 copy-start.6
  107.3 1.3 copy-start.11
  113.0 340.2 %reduce-scatter.5.cloned.1.call-start = ((), (), s32[]{:S(2)}) async-start(), calls=%async_computation.4 | async-start | bytes 540672 | tf_op jit(solution)/shard_map/reduce_scatter | solution.py:88
  229.4 1.5 copy-start.9
  231.0 2.5 copy-start.7
  231.0 2.5 copy-start.8
  232.5 0.8 copy-start.1
  232.5 1.0 copy-start.3
  235.1 440.5 %reduce-scatter.3.cloned.1.call-start = ((), (), s32[]{:S(2)}) async-start(), calls=%async_computation.3 | async-start | bytes 540672 | tf_op jit(solution)/shard_map/reduce_scatter | solution.py:74
  237.6 2.6 copy-start.2
  237.6 2.6 copy-start.4
  241.9 211.2 %copy-start.10 = (bf16[16,512]{1,0:T(8,128)(2,1)S(1)}, bf16[16,512]{1,0:T(8,128)(2,1)}, u32[]{:S(2)}) copy-start(bf16[16,512]{1,0:T(8,128)(2,1)} %param.9) | copy-start | bytes 49156
Sparse Core Ops, SparseCore 0:
  113.1 116.3 all-reduce.2
  235.2 217.9 reduce-scatter.4
  458.1 217.3 reduce-scatter.2
